TPU v7x, 256 devices: a whole 4x4x8 slice. The times are simulated.
256 devices in a mesh: blk: 16 (over z, x_lo), head: 4 (over x_hi, core), batch: 4 (over y).
Axes of the slice: x: 4 (x_hi: 2, x_lo: 2; x = x_hi * 2 + x_lo), y: 4, z: 8, core: 2. Of those that a mesh axis runs over, the one named last changes fastest.
Arguments:
- query_rows: bfloat16 [16384, 3072], P(('batch', 'blk'), 'head'), parts along dimension 0, may hold values from -6 to 6
- key_rows: bfloat16 [16384, 3072], P(('batch', 'blk'), 'head'), parts along dimension 0, may hold values from -6 to 6
- value_rows: bfloat16 [16384, 3072], P(('batch', 'blk'), 'head'), parts along dimension 0, may hold values from -6 to 6
- query_tangent: bfloat16 [16384, 3072], P(('batch', 'blk'), 'head'), parts along dimension 0, may hold values from -6 to 6
- key_tangent: bfloat16 [16384, 3072], P(('batch', 'blk'), 'head'), parts along dimension 0, may hold values from -6 to 6
- value_tangent: bfloat16 [16384, 3072], P(('batch', 'blk'), 'head'), parts along dimension 0, may hold values from -6 to 6
Outputs:
- attended: bfloat16 [16384, 3072], P(('batch', 'blk', 'head')), parts along dimension 0
- attended_tangent: bfloat16 [16384, 3072], P(('batch', 'blk', 'head')), parts along dimension 0
There are 4 independent parts, one for each index of `batch`. A program takes and returns all parts, laid end to end along the dimension named above; each array names one. Nothing has to cross between parts.
All inputs are finite; a program needn't handle non-finite values.
Results may differ from a plain program's by a relative error of at most 0.011.
Values may be sent and summed in bfloat16 or wider, within the bound.
A program may use at most 128 MiB of HBM per device.

v0:
```python
from functools import partial

import jax
import jax.numpy as jnp
from jax import lax
from jax.sharding import PartitionSpec as P

HD = 128


LOWEST = -1e30


def score_pair(query_heads, tangent_heads, key_block, key_change, scaling):
    scores = (
        jnp.einsum("qhd,khd->qhk", query_heads, key_block, preferred_element_type=jnp.float32)
        * scaling
    )
    score_change = (
        jnp.einsum("qhd,khd->qhk", tangent_heads, key_block, preferred_element_type=jnp.float32)
        + jnp.einsum("qhd,khd->qhk", query_heads, key_change, preferred_element_type=jnp.float32)
    ) * scaling
    return (scores, score_change)


def block_update(running, members, query_heads, tangent_heads, scaling):
    row_max, row_total, row_shift, numerator, tangent_numerator = running
    key_block, value_block, key_change, value_change = members
    scores, score_change = score_pair(query_heads, tangent_heads, key_block, key_change, scaling)
    new_max = jnp.maximum(row_max, jnp.max(scores, axis=2))
    shrink = jnp.exp(row_max - new_max)
    weights = jnp.exp(scores - new_max[:, :, None])
    mixed_terms = weights * score_change
    row_total = row_total * shrink + jnp.sum(weights, axis=2)
    row_shift = row_shift * shrink + jnp.sum(mixed_terms, axis=2)
    weights_low = weights.astype(jnp.bfloat16)
    mixed_low = mixed_terms.astype(jnp.bfloat16)
    numerator = numerator * shrink[:, :, None] + jnp.einsum(
        "qhk,khd->qhd", weights_low, value_block, preferred_element_type=jnp.float32
    )
    tangent_numerator = (
        tangent_numerator * shrink[:, :, None]
        + jnp.einsum("qhk,khd->qhd", mixed_low, value_block, preferred_element_type=jnp.float32)
        + jnp.einsum("qhk,khd->qhd", weights_low, value_change, preferred_element_type=jnp.float32)
    )
    return (new_max, row_total, row_shift, numerator, tangent_numerator)


def fold_keys(running, pieces, start, query_heads, tangent_heads):
    key_count = pieces[0].shape[0]
    head_count = query_heads.shape[1]
    head_width = query_heads.shape[2]
    block_rows = key_count
    while block_rows > 1024 and block_rows % 2 == 0:
        block_rows = block_rows // 2
    stacked = tuple(
        (
            member.reshape(key_count // block_rows, block_rows, head_count, head_width)
            for member in pieces
        )
    )
    scaling = head_width ** (-0.5)

    def advance(carried, members):
        return (block_update(carried, members, query_heads, tangent_heads, scaling), None)

    running, unused = lax.scan(advance, running, stacked)
    return running


def prepare(query_rows, query_tangent):
    query_heads = query_rows.reshape(query_rows.shape[0], -1, HD)
    tangent_heads = query_tangent.reshape(query_tangent.shape[0], -1, HD)
    rows_here = query_heads.shape[0]
    head_count = query_heads.shape[1]
    zero_stats = jnp.zeros((rows_here, head_count), jnp.float32)
    zero_rows = jnp.zeros((rows_here, head_count, HD), jnp.float32)
    initial = (
        jnp.full((rows_here, head_count), LOWEST, jnp.float32),
        zero_stats,
        zero_stats,
        zero_rows,
        zero_rows,
    )
    folder = partial(fold_keys, query_heads=query_heads, tangent_heads=tangent_heads)
    return (folder, initial)


def finish(running):
    row_max, row_total, row_shift, numerator, tangent_numerator = running
    attended = numerator / row_total[:, :, None]
    attended_tangent = (
        tangent_numerator / row_total[:, :, None] - (row_shift / row_total)[:, :, None] * attended
    )
    rows_here = attended.shape[0]
    return (
        attended.reshape(rows_here, -1).astype(jnp.bfloat16),
        attended_tangent.reshape(rows_here, -1).astype(jnp.bfloat16),
    )


def local(query_rows, key_rows, value_rows, query_tangent, key_tangent, value_tangent):
    folder, initial = prepare(query_rows, query_tangent)
    running = folder(
        initial,
        (
            lax.all_gather(key_rows, "blk", axis=0, tiled=True),
            lax.all_gather(value_rows, "blk", axis=0, tiled=True),
            lax.all_gather(key_tangent, "blk", axis=0, tiled=True),
            lax.all_gather(value_tangent, "blk", axis=0, tiled=True),
        ),
        jnp.int32(0),
    )
    result_rows, result_tangent = finish(running)
    attended, attended_tangent = (
        lax.all_to_all(result_rows, "head", split_axis=0, concat_axis=1, tiled=True),
        lax.all_to_all(result_tangent, "head", split_axis=0, concat_axis=1, tiled=True),
    )
    return (attended, attended_tangent)


def solution(mesh):
    return jax.shard_map(
        local,
        mesh=mesh,
        in_specs=(
            P(("batch", "blk"), "head"),
            P(("batch", "blk"), "head"),
            P(("batch", "blk"), "head"),
            P(("batch", "blk"), "head"),
            P(("batch", "blk"), "head"),
            P(("batch", "blk"), "head"),
        ),
        out_specs=(P(("batch", "blk", "head"), None), P(("batch", "blk", "head"), None)),
        check_vma=False,
    )
```

profile of v0, /device:TPU:1, one launch (start us, length us, event | category | flops | bytes accessed | tf_op | source)
XLA Modules:
  0.0 715.6 jit_solution(13581352506316343537)
XLA Ops:
  12.8 141.1 %all-gather.5.cloned.1.call-done = bf16[4096,768]{1,0:T(8,128)(2,1)} async-done(((bf16[256,768]{1,0:T(8,128)(2,1)}), bf16[4096,768]{1,0:T(8,128)(2,1)}) %all-gather.5.cloned.1.call-update) | async-done | bytes 6291472 | tf_op jit(solution)/shard_map/all_gather | solution.py:107
  153.9 13.7 %reshape.44 = bf16[4,1024,6,128]{3,2,1,0:T(8,128)(2,1)} reshape(bf16[4096,768]{1,0:T(8,128)(2,1)} %all-gather.5.cloned.1.call-done) | data formatting | bytes 12582912 | tf_op jit(solution)/shard_map/reshape | solution.py:58
  167.6 7.5 %copy.39 = bf16[4,1024,6,128]{3,1,2,0:T(8,128)(2,1)} copy(bf16[4,1024,6,128]{3,2,1,0:T(8,128)(2,1)} %reshape.44) | data formatting | bytes 12582912
  175.1 121.9 %all-gather.7.cloned.1.call-done = bf16[4096,768]{1,0:T(8,128)(2,1)} async-done(((bf16[256,768]{1,0:T(8,128)(2,1)}), bf16[4096,768]{1,0:T(8,128)(2,1)}) %all-gather.7.cloned.1.call-update) | async-done | bytes 6291472 | tf_op jit(solution)/shard_map/all_gather | solution.py:109
  297.0 13.7 %reshape.45 = bf16[4,1024,6,128]{3,2,1,0:T(8,128)(2,1)} reshape(bf16[4096,768]{1,0:T(8,128)(2,1)} %all-gather.7.cloned.1.call-done) | data formatting | bytes 12582912 | tf_op jit(solution)/shard_map/reshape | solution.py:58
  310.7 7.5 %copy.42 = bf16[4,1024,6,128]{3,1,2,0:T(8,128)(2,1)} copy(bf16[4,1024,6,128]{3,2,1,0:T(8,128)(2,1)} %reshape.45) | data formatting | bytes 12582912
  318.2 121.9 %all-gather.9.cloned.1.call-done = bf16[4096,768]{1,0:T(8,128)(2,1)} async-done(((bf16[256,768]{1,0:T(8,128)(2,1)}), bf16[4096,768]{1,0:T(8,128)(2,1)}) %all-gather.9.cloned.1.call-update) | async-done | bytes 6291472 | tf_op jit(solution)/shard_map/all_gather | solution.py:108
  440.1 13.7 %reshape.46 = bf16[4,1024,6,128]{3,2,1,0:T(8,128)(2,1)} reshape(bf16[4096,768]{1,0:T(8,128)(2,1)} %all-gather.9.cloned.1.call-done) | data formatting | bytes 12582912 | tf_op jit(solution)/shard_map/reshape | solution.py:58
  453.8 11.5 %copy.43 = bf16[4,1024,6,128]{1,3,2,0:T(8,128)(2,1)} copy(bf16[4,1024,6,128]{3,2,1,0:T(8,128)(2,1)} %reshape.46) | data formatting | bytes 12582912
  465.3 117.8 %all-gather.11.cloned.1.call-done = bf16[4096,768]{1,0:T(8,128)(2,1)} async-done(((bf16[256,768]{1,0:T(8,128)(2,1)}), bf16[4096,768]{1,0:T(8,128)(2,1)}) %all-gather.11.cloned.1.call-update) | async-done | bytes 6291472 | tf_op jit(solution)/shard_map/all_gather | solution.py:110
  583.0 13.7 %reshape.47 = bf16[4,1024,6,128]{3,2,1,0:T(8,128)(2,1)} reshape(bf16[4096,768]{1,0:T(8,128)(2,1)} %all-gather.11.cloned.1.call-done) | data formatting | bytes 12582912 | tf_op jit(solution)/shard_map/reshape | solution.py:58
  596.7 11.4 %copy.44 = bf16[4,1024,6,128]{1,3,2,0:T(8,128)(2,1)} copy(bf16[4,1024,6,128]{3,2,1,0:T(8,128)(2,1)} %reshape.47) | data formatting | bytes 12582912
  608.1 72.6 %while.19 = (s32[]{:T(128)}, f32[256,6]{0,1:T(8,128)S(1)}, f32[256,6]{0,1:T(8,128)S(1)}, f32[256,6]{0,1:T(8,128)S(1)}, f32[256,6,128]{0,2,1:T(8,128)S(1)}, /*ind...) while((s32[]{:T(128)}, f32[256,6]{0,1:T(8,128)S(1)}, ...), condition=%wide.region_4.5_spmd.clone, body=%wide.region_0.4_spmd.clone.sunk | while | flops 2445617664 | bytes 109863144 | solution.py:67
  608.1 5.0 bitcast_reduce_fusion.2
  626.3 5.1 bitcast_reduce_fusion.2
  634.6 4.0 fusion.91
  644.4 5.1 bitcast_reduce_fusion.2
  652.7 4.0 fusion.91
  662.6 5.1 bitcast_reduce_fusion.2
  670.9 4.0 fusion.91
  682.5 5.3 all-to-all-start
  689.4 6.5 all-to-all-done
  695.9 4.3 all-to-all-start.1
  701.0 7.3 %all-to-all-done.1 = bf16[4,64,768]{2,1,0:T(8,128)(2,1)S(1)} async-done(((bf16[4,64,768]{2,1,0:T(8,128)(2,1)}), bf16[4,64,768]{2,1,0:T(8,128)(2,1)S(1)}, u32[]{:S(2)}, u32[]{:S(2)}) %all-to-all-start.1) | async-done | bytes 393248 | tf_op jit(solution)/shard_map/all_to_all | solution.py:117
  (90 shorter events, 50.2 us)
Async XLA Ops:
  7.2 146.8 %all-gather.5.cloned.1.call-start = ((), (), s32[]{:S(2)}) async-start(), calls=%async_computation.2 | async-start | bytes 6684672 | tf_op jit(solution)/shard_map/all_gather | solution.py:107
  7.9 289.1 %all-gather.7.cloned.1.call-start = ((), (), s32[]{:S(2)}) async-start(), calls=%async_computation.3 | async-start | bytes 6684672 | tf_op jit(solution)/shard_map/all_gather | solution.py:109
  8.6 431.4 %all-gather.9.cloned.1.call-start = ((), (), s32[]{:S(2)}) async-start(), calls=%async_computation.4 | async-start | bytes 6684672 | tf_op jit(solution)/shard_map/all_gather | solution.py:108
  9.4 573.6 %all-gather.11.cloned.1.call-start = ((), (), s32[]{:S(2)}) async-start(), calls=%async_computation.5 | async-start | bytes 6684672 | tf_op jit(solution)/shard_map/all_gather | solution.py:110
  613.2 3.3 copy-start
  613.2 7.3 %slice-start = ((s8[6291456]{0:T(1024)(128)(4,1)}), s8[4194304]{0:T(1024)(128)(4,1)S(1)}, s32[]{:S(2)}) async-start(s8[6291456]{0:T(1024)(128)(4,1)} %bitcast.105), calls=%async_computation.6 | async-start | bytes 8388608 | tf_op jit(solution)/shard_map/while
  616.5 4.1 slice-start.1
  631.3 3.3 copy-start
  631.3 7.3 %slice-start = ((s8[6291456]{0:T(1024)(128)(4,1)}), s8[4194304]{0:T(1024)(128)(4,1)S(1)}, s32[]{:S(2)}) async-start(s8[6291456]{0:T(1024)(128)(4,1)} %bitcast.105), calls=%async_computation.6 | async-start | bytes 8388608 | tf_op jit(solution)/shard_map/while
  634.6 4.1 slice-start.1
  649.5 3.3 copy-start
  649.5 7.3 %slice-start = ((s8[6291456]{0:T(1024)(128)(4,1)}), s8[4194304]{0:T(1024)(128)(4,1)S(1)}, s32[]{:S(2)}) async-start(s8[6291456]{0:T(1024)(128)(4,1)} %bitcast.105), calls=%async_computation.6 | async-start | bytes 8388608 | tf_op jit(solution)/shard_map/while
  652.7 4.1 slice-start.1
  667.6 3.3 copy-start
  667.6 7.3 %slice-start = ((s8[6291456]{0:T(1024)(128)(4,1)}), s8[4194304]{0:T(1024)(128)(4,1)S(1)}, s32[]{:S(2)}) async-start(s8[6291456]{0:T(1024)(128)(4,1)} %bitcast.105), calls=%async_computation.6 | async-start | bytes 8388608 | tf_op jit(solution)/shard_map/while
  670.9 4.1 slice-start.1
  682.5 13.4 %all-to-all-start = ((bf16[4,64,768]{2,1,0:T(8,128)(2,1)}), bf16[4,64,768]{2,1,0:T(8,128)(2,1)S(1)}, u32[]{:S(2)}, u32[]{:S(2)}) async-start(bf16[4,64,768]{2,1,0:T(8,128)(2,1)} %convert_element_type.21), calls=%async_computation | async-start | bytes 786432 | tf_op jit(solution)/shard_map/all_to_all | solution.py:116
  695.9 12.4 %all-to-all-start.1 = ((bf16[4,64,768]{2,1,0:T(8,128)(2,1)}), bf16[4,64,768]{2,1,0:T(8,128)(2,1)S(1)}, u32[]{:S(2)}, u32[]{:S(2)}) async-start(bf16[4,64,768]{2,1,0:T(8,128)(2,1)} %convert_element_type.23), calls=%async_computation.1 | async-start | bytes 786432 | tf_op jit(solution)/shard_map/all_to_all | solution.py:117
Sparse Core Ops, SparseCore 0:
  9.8 144.0 all-gather.4
  155.7 141.2 all-gather.6
  298.8 141.2 all-gather.8
  441.7 141.2 all-gather.10
where the time goes:
time: 718 us; the launch traced here: 716 us
  waiting for transfers between devices  519 us (72%)
  local copies, waits for them, and re-layouts  103 us (14%)
  matrix products  65.1 us (9%)
  between operations  13.9 us (2%)
  starting transfers between devices  9.79 us (1%)
    all_gather x1, waiting for transfers between devices, local(): lax.all_gather(key_rows, 'blk', axis=0, tiled=True)  141 us
    all_gather x1, waiting for transfers between devices, local(): lax.all_gather(value_rows, 'blk', axis=0, tiled=True)  122 us
    all_gather x1, waiting for transfers between devices, local(): lax.all_gather(key_tangent, 'blk', axis=0, tiled=True)  122 us
    all_gather x1, waiting for transfers between devices, local(): lax.all_gather(value_tangent, 'blk', axis=0, tiled=True)  118 us
    reshape x4, local copies, waits for them, and re-layouts, fold_keys(): member.reshape(key_count // block_rows, block_rows, head_count, head_width)  54.7 us
    unnamed x8, local copies, waits for them, and re-layouts  40.7 us
    dot_general x4, matrix products, score_pair(): jnp.einsum('qhd,khd->qhk', query_heads, key_block, preferred_element_type...  20.2 us
    dot_general x4, matrix products, score_pair(): jnp.einsum('qhd,khd->qhk', query_heads, key_change, preferred_element_typ...  16.1 us
  transfers between devices with their start and end apart: 6, of which 6 were waited for; matrix products, arithmetic and copies ran while one was open for 10% of the time, Pallas kernels for 0%

commit v1 on v0

v1 whole, which is shorter than its diff:
```python
import functools

import jax
import jax.numpy as jnp
from jax import lax
from jax.experimental import pallas as pl
from jax.experimental.pallas import tpu as pltpu
from jax.sharding import PartitionSpec as P

HD = 128
MESH = pl.DeviceIdType.MESH
LOWEST = -1e30
LOG2E = 1.4426950408889634
NT = (((1,), (1,)), ((), ()))

NZ = 8
OWN = 6


def owner_z(i, column):
    return lax.rem(i + i // 3 + 2 * column, NZ)


def kernel(
    rows, q_in, k_in, v_in, qt_in, kt_in, vt_in, o_ref, ot_ref,
    qq, kk, vv, acc, acct, top, total, shift, res,
    send_in, got_q, got_k, got_v, pass_k, pass_v, come_k, come_v, send_out, got_out,
):
    quarter = rows // 4
    blk, head, y = lax.axis_index("blk"), lax.axis_index("head"), lax.axis_index("batch")
    z, s = blk // 2, lax.rem(blk, 2)
    x_hi, core = head // 2, lax.rem(head, 2)
    place = lax.rem(z + NZ - 2 * s, NZ)
    active = lax.rem(place, 4) != 3
    mine = place - place // 4
    at_home = jnp.logical_and(active, s == core)

    def device(to_blk, to_head):
        return (to_blk, to_head, y)

    barrier = pltpu.get_barrier_semaphore()

    def greet(to_blk, to_head):
        pl.semaphore_signal(barrier, inc=1, device_id=device(to_blk, to_head), device_id_type=MESH)

    @pl.when(active)
    def _():
        greet(blk, 2 * x_hi + 1 - core)

        @pl.loop(0, NZ)
        def _(j):
            @pl.when(jnp.logical_not(jnp.logical_and(j == z, s == core)))
            def _():
                greet(2 * j + core, 2 * x_hi + s)

    @pl.loop(0, OWN)
    def _(i):
        for column in range(2):
            for half in range(2):
                zo = owner_z(i, column)
                to_blk, to_head = 2 * zo + column, 2 * half + s

                @pl.when(jnp.logical_not(jnp.logical_and(to_blk == blk, to_head == head)))
                def _():
                    greet(to_blk, to_head)

    expected = jnp.where(active, OWN + 1 + 32, OWN) - jnp.where(at_home, 2, 0)
    pl.semaphore_wait(barrier, expected)

    def each_owner(act):
        @pl.loop(0, OWN)
        def _(n):
            i = lax.rem(n + z, OWN)
            act(i, owner_z(i, core))

    def send(i, zo, a, src_ref, dst_ref, got):
        src = src_ref.at[:, pl.ds(pl.multiple_of(i * HD, HD), HD)]
        here = jnp.logical_and(zo == z, s == core)

        @pl.when(here)
        def _():
            pltpu.make_async_copy(src, dst_ref, got).start()

        @pl.when(jnp.logical_not(here))
        def _():
            pltpu.make_async_remote_copy(
                src_ref=src, dst_ref=dst_ref, send_sem=send_in.at[a, i], recv_sem=got,
                device_id=device(2 * zo + core, 2 * x_hi + s), device_id_type=MESH,
            ).start()

    def send_queries(i, zo):
        send(i, zo, 0, qt_in, qq.at[z, :, 0:HD], got_q.at[z])
        send(i, zo, 1, q_in, qq.at[z, :, HD:2 * HD], got_q.at[z])

    def send_keys(i, zo):
        send(i, zo, 2, k_in, kk.at[s, z, :, 0:HD], got_k.at[z])
        send(i, zo, 3, kt_in, kk.at[s, z, :, HD:2 * HD], got_k.at[z])
        send(i, zo, 4, v_in, vv.at[s, z, :, 0:HD], got_v.at[z])
        send(i, zo, 5, vt_in, vv.at[s, z, :, HD:2 * HD], got_v.at[z])

    each_owner(send_queries)
    each_owner(send_keys)

    scaling = HD ** -0.5
    factor = scaling * LOG2E

    def attend(j, kb, vb):
        at = pl.ds(pl.multiple_of(j * rows, rows), rows)
        both = qq[j]
        keys = kb[...]
        scores = lax.dot_general(both[:, HD:], keys[:, :HD], NT, preferred_element_type=jnp.float32)
        change = lax.dot_general(both, keys, NT, preferred_element_type=jnp.float32)
        old = top[at, :]
        new = jnp.maximum(old, jnp.max(scores, axis=1, keepdims=True))
        shrink = jnp.exp2((old - new) * factor)
        weights = jnp.exp2((scores - new[:, :1]) * factor)
        mixed = weights * change
        top[at, :] = new
        total[at, :] = total[at, :] * shrink + jnp.sum(weights, axis=1, keepdims=True)
        shift[at, :] = shift[at, :] * shrink + jnp.sum(mixed, axis=1, keepdims=True)
        values = vb[...]
        shrinks = jnp.concatenate([shrink, shrink], axis=1)
        acc[at, :] = acc[at, :] * shrinks + jnp.dot(
            weights.astype(jnp.bfloat16), values, preferred_element_type=jnp.float32)
        acct[at, :] = acct[at, :] * shrink + jnp.dot(
            mixed.astype(jnp.bfloat16), values[:, :HD], preferred_element_type=jnp.float32)

    def to_sibling(j, src, send_sem, recv_sem):
        return pltpu.make_async_remote_copy(
            src_ref=src.at[core, j], dst_ref=src.at[core, j], send_sem=send_sem.at[j], recv_sem=recv_sem.at[j],
            device_id=device(blk, 2 * x_hi + 1 - core), device_id_type=MESH,
        )

    def landed(ref, sem):
        pltpu.make_async_copy(ref, ref, sem).wait()

    column0 = (2 * x_hi + s) * OWN + mine
    out_columns = pl.ds(pl.multiple_of(column0 * HD, HD), HD)

    def send_result(j):
        for part in range(4):
            piece = pl.ds(pl.multiple_of(j * rows + part * quarter, quarter), quarter)
            here = jnp.logical_and(2 * j + core == blk, head == part)
            for a, out in ((0, o_ref), (1, ot_ref)):
                src = res.at[a, piece, :]
                dst = out.at[:, out_columns]

                @pl.when(here)
                def _():
                    pltpu.make_async_copy(src, dst, got_out.at[a]).start()

                @pl.when(jnp.logical_not(here))
                def _():
                    pltpu.make_async_remote_copy(
                        src_ref=src, dst_ref=dst, send_sem=send_out.at[a, j, part], recv_sem=got_out.at[a],
                        device_id=device(2 * j + core, part), device_id_type=MESH,
                    ).start()

    def finish(j):
        at = pl.ds(pl.multiple_of(j * rows, rows), rows)
        inverse = 1.0 / total[at, :]
        attended = acc[at, 0:HD] * inverse
        tangent = (acct[at, :] * scaling + acc[at, HD:2 * HD]) * inverse
        tangent = tangent - (shift[at, :] * scaling * inverse) * attended
        res[0, at, :] = attended.astype(jnp.bfloat16)
        res[1, at, :] = tangent.astype(jnp.bfloat16)

    @pl.when(active)
    def _():
        top[...] = jnp.full_like(top, LOWEST)
        total[...] = jnp.zeros_like(total)
        shift[...] = jnp.zeros_like(shift)
        acc[...] = jnp.zeros_like(acc)
        acct[...] = jnp.zeros_like(acct)

        @pl.loop(0, NZ)
        def _(j):
            landed(qq.at[j], got_q.at[j])

        @pl.loop(0, NZ)
        def _(n):
            b = lax.rem(z + n, NZ)
            landed(kk.at[core, b], got_k.at[b])
            to_sibling(b, kk, pass_k, come_k).start()
            landed(vv.at[core, b], got_v.at[b])
            to_sibling(b, vv, pass_v, come_v).start()

            @pl.loop(0, NZ)
            def _(j):
                attend(j, kk.at[core, b], vv.at[core, b])

            landed(kk.at[1 - core, b], come_k.at[b])
            landed(vv.at[1 - core, b], come_v.at[b])

            @pl.loop(0, NZ)
            def _(m):
                j = lax.rem(m + z, NZ)
                attend(j, kk.at[1 - core, b], vv.at[1 - core, b])

                @pl.when(n == NZ - 1)
                def _():
                    finish(j)
                    send_result(j)

    def sent(i, zo):
        @pl.when(jnp.logical_not(jnp.logical_and(zo == z, s == core)))
        def _():
            for a, src_ref in enumerate((qt_in, q_in, k_in, kt_in, v_in, vt_in)):
                src = src_ref.at[:, pl.ds(pl.multiple_of(i * HD, HD), HD)]
                pltpu.make_async_copy(src, src, send_in.at[a, i]).wait()

    each_owner(sent)

    @pl.when(active)
    def _():
        @pl.loop(0, NZ)
        def _(j):
            landed(kk.at[core, j], pass_k.at[j])
            landed(vv.at[core, j], pass_v.at[j])
            for part in range(4):
                piece = pl.ds(pl.multiple_of(j * rows + part * quarter, quarter), quarter)

                @pl.when(jnp.logical_not(jnp.logical_and(2 * j + core == blk, head == part)))
                def _():
                    for a in range(2):
                        landed(res.at[a, piece, :], send_out.at[a, j, part])

    landed(o_ref, got_out.at[0])
    landed(ot_ref, got_out.at[1])


def local(*arrays):
    rows = arrays[0].shape[0]
    out = jax.ShapeDtypeStruct((rows // 4, 24 * HD), jnp.bfloat16)
    queries = NZ * rows
    f32 = jnp.float32
    dma = pltpu.SemaphoreType.DMA
    return tuple(pl.pallas_call(
        functools.partial(kernel, rows),
        out_shape=(out, out),
        in_specs=[pl.BlockSpec(memory_space=pl.ANY)] * 6,
        out_specs=(pl.BlockSpec(memory_space=pltpu.VMEM),) * 2,
        scratch_shapes=[
            pltpu.VMEM((NZ, rows, 2 * HD), jnp.bfloat16),
            pltpu.VMEM((2, NZ, rows, 2 * HD), jnp.bfloat16),
            pltpu.VMEM((2, NZ, rows, 2 * HD), jnp.bfloat16),
            pltpu.VMEM((queries, 2 * HD), f32),
            pltpu.VMEM((queries, HD), f32),
            pltpu.VMEM((queries, HD), f32),
            pltpu.VMEM((queries, HD), f32),
            pltpu.VMEM((queries, HD), f32),
            pltpu.VMEM((2, queries, HD), jnp.bfloat16),
            dma((6, OWN)), dma((NZ,)), dma((NZ,)), dma((NZ,)),
            dma((NZ,)), dma((NZ,)), dma((NZ,)), dma((NZ,)),
            dma((2, NZ, 4)), dma((2,)),
        ],
        compiler_params=pltpu.CompilerParams(
            collective_id=0, has_side_effects=True, vmem_limit_bytes=48 * 2**20),
        name="attention_tangent",
    )(*arrays))


def solution(mesh):
    rows_in = P(("batch", "blk"), "head")
    rows_out = P(("batch", "blk", "head"), None)
    return jax.shard_map(
        local, mesh=mesh, in_specs=(rows_in,) * 6, out_specs=(rows_out, rows_out), check_vma=False,
    )
```

time: 718 us -> 152 us (0.21)
  waiting for transfers between devices: 519 us -> 0 us
  Pallas kernels: 0 us -> 141 us
  local copies, waits for them, and re-layouts: 103 us -> 7.46 us
  matrix products: 65.1 us -> 0 us
  between operations: 13.9 us -> 0.65 us
  starting transfers between devices: 9.79 us -> 0 us
    all_gather x4 -> x0, waiting for transfers between devices: 503 us -> none  [the longest x1 141 us: local(): lax.all_gather(key_rows, 'blk', axis=0, tiled=True)]
    pallas_call x0 -> x1, Pallas kernels: none -> 141 us  [local(): pl.pallas_call(functools.partial(kernel, rows), out_shape=(out, out), in_...]
    dot_general x24 -> x0, matrix products: 65.1 us -> none  [the longest x4 20.2 us: score_pair(): jnp.einsum('qhd,khd->qhk', query_heads, key_block, preferred_element_type...]
    reshape x4 -> x0, local copies, waits for them, and re-layouts: 54.7 us -> none  [fold_keys(): member.reshape(key_count // block_rows, block_rows, head_count, head_width)]
    unnamed x8 -> x14, local copies, waits for them, and re-layouts: 40.7 us -> 7.46 us
    all_to_all x2 -> x0, waiting for transfers between devices: 13.8 us -> none  [the longest x1 7.3 us: local(): lax.all_to_all(result_tangent, 'head', split_axis=0, concat_axis=1, tiled...]
    all_to_all x2 -> x0, starting transfers between devices: 9.64 us -> none  [the longest x1 5.34 us: local(): lax.all_to_all(result_rows, 'head', split_axis=0, concat_axis=1, tiled=True)]
  transfers between devices with their start and end apart: 6 -> 0, of which waited for: 6 -> 0; matrix products, arithmetic and copies ran while one was open for 10% -> 0% of each run, Pallas kernels for 0% -> 0%
where the time goes in v1:
time: 152 us; the launch traced here: 149 us
  Pallas kernels  141 us (93%)
  local copies, waits for them, and re-layouts  7.46 us (5%)
    pallas_call x1, Pallas kernels, local(): pl.pallas_call(functools.partial(kernel, rows), out_shape=(out, out), in_...  141 us
    unnamed x14, local copies, waits for them, and re-layouts  7.46 us

profile of v1, /device:TPU:1, one launch (start us, length us, event | category | flops | bytes accessed | tf_op | source)
XLA Modules:
  0.0 149.2 jit_solution(16854015454918924794)
XLA Ops:
  0.6 0.0 copy-start
  0.6 1.0 copy-done
  1.6 0.0 copy-start.1
  1.6 1.0 copy-done.1
  2.6 0.0 copy-start.2
  2.6 1.0 copy-done.2
  3.6 0.0 copy-start.3
  3.6 1.0 copy-done.3
  4.6 0.0 copy-start.4
  4.6 1.0 copy-done.4
  5.6 0.0 copy-start.5
  5.6 1.0 copy-done.5
  6.6 141.0 %attention_tangent.1 = (bf16[64,3072]{1,0:T(8,128)(2,1)S(1)}, bf16[64,3072]{1,0:T(8,128)(2,1)S(1)}) custom-call(bf16[256,768]{1,0:T(8,128)(2,1)S(1)} %copy-done, bf16[256,768]{1,0:T(8,128)(2,1)S(1)} %copy-done.1, bf16[256,768]{1,0:T(8,128)(2,1)S(1)} %copy-done.2, bf16[256,768]{1,0:T(8,128)(2,1)S(1)} %copy-done.3, bf16[256,768]{1,0:T(8,128)(2,1)S(1)} %copy-done.4, ...), custom_call_target="tpu_custom_call" | custom-call | tf_op jit(solution)/shard_map/attention_tangent/pallas_call | solution.py:238
  147.7 0.7 copy.10
  148.4 0.7 copy.11
Async XLA Ops:
  0.6 1.0 copy-start
  1.6 1.0 copy-start.1
  2.6 1.0 copy-start.2
  3.6 1.0 copy-start.3
  4.6 1.0 copy-start.4
  5.6 1.0 copy-start.5

commit v2 on v1

v2 whole, which is shorter than its diff:
```python
import functools

import jax
import jax.numpy as jnp
from jax import lax
from jax.experimental import pallas as pl
from jax.experimental.pallas import tpu as pltpu
from jax.sharding import PartitionSpec as P

HD = 128
MESH = pl.DeviceIdType.MESH
LOG2E = 1.4426950408889634
NT = (((1,), (1,)), ((), ()))

NZ = 8
MANY = 2048
OWN = 6


def step_of(n, turn):
    away = (3 - (n - 2) // 2) * (1 - 2 * (n % 2))
    return turn * (0 if n == 0 else 4 if n == 1 else away)


def step_at(n, turn):
    away = (3 - (n - 2) // 2) * (1 - 2 * lax.rem(n, 2))
    return turn * jnp.where(n == 0, 0, jnp.where(n == 1, 4, away))


def kernel(
    rows, q_in, k_in, v_in, qt_in, kt_in, vt_in, o_ref, ot_ref,
    qq, kk, vv, res, got,
    send_in, got_q, got_k, got_v, pass_k, pass_v, come_k, come_v, send_out, got_out,
):
    quarter = rows // 4
    blk, head, y = lax.axis_index("blk"), lax.axis_index("head"), lax.axis_index("batch")
    z, s = blk // 2, lax.rem(blk, 2)
    x_hi, core = head // 2, lax.rem(head, 2)
    place = lax.rem(z + NZ - 2 * s, NZ)
    active = lax.rem(place, 4) != 3
    mine = place - place // 4
    at_home = jnp.logical_and(active, s == core)

    def device(to_blk, to_head):
        return (to_blk, to_head, y)

    barrier = pltpu.get_barrier_semaphore()

    def greet(to_blk, to_head):
        pl.semaphore_signal(barrier, inc=1, device_id=device(to_blk, to_head), device_id_type=MESH)

    @pl.when(active)
    def _():
        @pl.loop(0, NZ)
        def _(j):
            @pl.when(jnp.logical_not(jnp.logical_and(j == z, s == core)))
            def _():
                greet(2 * j + core, 2 * x_hi + s)

    for other in range(1, 4):
        greet(blk, lax.rem(head + other, 4))
    pl.semaphore_wait(barrier, OWN + 3 - jnp.where(at_home, 1, 0))

    sources = (qt_in, q_in, k_in, kt_in, v_in, vt_in)
    turn = 1 - 2 * core

    def owner_at(n):
        zo = lax.rem(z + step_of(n, turn) + NZ, NZ)
        there = lax.rem(zo + NZ - 2 * core, NZ)
        return zo, there - there // 4, lax.rem(there, 4) != 3

    def slot(n, side):
        return pl.ds(pl.multiple_of((2 * n + side) * rows, rows), rows)

    def send(n, a):
        zo, i, owns = owner_at(n)
        src = sources[a].at[:, pl.ds(pl.multiple_of(i * HD, HD), HD)]
        half = slice(HD * (a % 2), HD * (a % 2 + 1))
        if a < 2:
            dst, got_sem = qq.at[n * rows:(n + 1) * rows, half], got_q.at[n]
        elif a < 4:
            dst, got_sem = kk.at[slot(n, s), half], got_k.at[n]
        else:
            dst, got_sem = vv.at[slot(n, s), half], got_v.at[n]

        def local():
            pltpu.make_async_copy(src, dst, got_sem).start()

        def remote():
            pltpu.make_async_remote_copy(
                src_ref=src, dst_ref=dst, send_sem=send_in.at[a, i], recv_sem=got_sem,
                device_id=device(2 * zo + core, 2 * x_hi + s), device_id_type=MESH,
            ).start()

        if n == 0:
            pl.when(jnp.logical_and(owns, s == core))(local)
            pl.when(jnp.logical_and(owns, s != core))(remote)
        else:
            pl.when(owns)(remote)

    for kinds, steps in (((0, 1), (0,)), ((2, 3, 4, 5), (0, 2, 4, 6)), ((0, 1), (2, 4, 6))):
        for n in steps:
            for a in kinds:
                send(n, a)
                send(n + 1, a)

    scaling = HD ** -0.5
    factor = scaling * LOG2E

    def wide(a, count):
        return jnp.concatenate([a] * count, axis=1)

    def lanes(a):
        parts = [a[:, c:c + HD] for c in range(0, a.shape[1], HD)]
        return functools.reduce(jnp.add, parts)

    def attend(n):
        both = qq[pl.ds(pl.multiple_of(n * rows, rows), rows), :]
        count = NZ * 2 * rows
        part = min(count, MANY)
        for c in range(0, count, part):
            keys, values = kk[c:c + part, :], vv[c:c + part, :]
            scores = lax.dot_general(both[:, HD:], keys[:, :HD], NT, preferred_element_type=jnp.float32)
            change = lax.dot_general(both, keys, NT, preferred_element_type=jnp.float32)
            peak = jnp.broadcast_to(jnp.max(scores, axis=1, keepdims=True), (rows, HD))
            new = peak if c == 0 else jnp.maximum(top, peak)
            weights = jnp.exp2((scores - wide(new, part // HD)) * factor)
            mixed = weights * change
            sums = lanes(weights), lanes(mixed)
            mix = jnp.dot(weights.astype(jnp.bfloat16), values, preferred_element_type=jnp.float32)
            mixt = jnp.dot(mixed.astype(jnp.bfloat16), values[:, :HD], preferred_element_type=jnp.float32)
            if c == 0:
                top, total, shift, acc, acct = new, *sums, mix, mixt
            else:
                shrink = jnp.exp2((top - new) * factor)
                top, total, shift = new, total * shrink + sums[0], shift * shrink + sums[1]
                acc, acct = acc * wide(shrink, 2) + mix, acct * shrink + mixt
        inverse = 1.0 / jnp.sum(total, axis=1, keepdims=True)
        shifted = jnp.sum(shift, axis=1, keepdims=True) * (scaling * inverse)
        attended = acc[:, :HD] * inverse
        tangent = (acct * scaling + acc[:, HD:]) * inverse - shifted * attended
        for a, result in ((0, attended), (1, tangent)):
            for p in range(4):
                res[n, p, a] = result[p * quarter:(p + 1) * quarter, :].astype(jnp.bfloat16)

    def to_sibling(n, ref, send_sem, recv_sem):
        mine = ref.at[slot(n, core), :]
        return pltpu.make_async_remote_copy(
            src_ref=mine, dst_ref=mine, send_sem=send_sem.at[n], recv_sem=recv_sem.at[n],
            device_id=device(blk, 2 * x_hi + 1 - core), device_id_type=MESH,
        )

    def landed(ref, sem):
        pltpu.make_async_copy(ref, ref, sem).wait()

    column0 = (2 * x_hi + s) * OWN + mine

    def row_home(n):
        return 2 * lax.rem(z - step_at(n, 1 - 2 * s) + NZ, NZ) + core

    def send_result(n):
        home = row_home(n)
        for part in range(4):
            src, dst = res.at[n, part], got.at[column0]
            here = jnp.logical_and(home == blk, head == part)

            @pl.when(here)
            def _():
                pltpu.make_async_copy(src, dst, got_out).start()

            @pl.when(jnp.logical_not(here))
            def _():
                pltpu.make_async_remote_copy(
                    src_ref=src, dst_ref=dst, send_sem=send_out.at[n, part], recv_sem=got_out,
                    device_id=device(home, part), device_id_type=MESH,
                ).start()

    @pl.when(active)
    def _():
        @pl.loop(0, NZ)
        def _(n):
            landed(kk.at[slot(n, core), :], got_k.at[n])
            to_sibling(n, kk, pass_k, come_k).start()
            landed(vv.at[slot(n, core), :], got_v.at[n])
            to_sibling(n, vv, pass_v, come_v).start()

        @pl.loop(0, NZ)
        def _(n):
            landed(kk.at[slot(n, 1 - core), :], come_k.at[n])
            landed(vv.at[slot(n, 1 - core), :], come_v.at[n])

        @pl.loop(0, NZ)
        def _(n):
            landed(qq.at[pl.ds(pl.multiple_of(n * rows, rows), rows), :], got_q.at[n])
            attend(n)
            send_result(n)

    for n in range(NZ):
        zo, i, owns = owner_at(n)
        src = q_in.at[:, pl.ds(pl.multiple_of(i * HD, HD), HD)]

        @pl.when(jnp.logical_and(owns, s != core) if n == 0 else owns)
        def _():
            for a in range(6):
                landed(src, send_in.at[a, i])

    @pl.when(active)
    def _():
        @pl.loop(0, NZ)
        def _(n):
            landed(kk.at[slot(n, core), :], pass_k.at[n])
            landed(vv.at[slot(n, core), :], pass_v.at[n])
            for part in range(4):
                @pl.when(jnp.logical_not(jnp.logical_and(row_home(n) == blk, head == part)))
                def _():
                    landed(res.at[n, part], send_out.at[n, part])

    landed(got, got_out)
    for h in range(4 * OWN):
        o_ref[:, h * HD:(h + 1) * HD] = got[h, 0]
        ot_ref[:, h * HD:(h + 1) * HD] = got[h, 1]


def local(*arrays):
    rows = arrays[0].shape[0]
    out = jax.ShapeDtypeStruct((rows // 4, 24 * HD), jnp.bfloat16)
    queries = NZ * rows
    bf16 = jnp.bfloat16
    dma = pltpu.SemaphoreType.DMA
    return tuple(pl.pallas_call(
        functools.partial(kernel, rows),
        out_shape=(out, out),
        in_specs=[pl.BlockSpec(memory_space=pltpu.HBM)] * 6,
        out_specs=(pl.BlockSpec(memory_space=pltpu.VMEM),) * 2,
        scratch_shapes=[
            pltpu.VMEM((queries, 2 * HD), bf16),
            pltpu.VMEM((2 * queries, 2 * HD), bf16),
            pltpu.VMEM((2 * queries, 2 * HD), bf16),
            pltpu.VMEM((NZ, 4, 2, rows // 4, HD), bf16),
            pltpu.VMEM((4 * OWN, 2, rows // 4, HD), bf16),
            dma((6, OWN)), dma((NZ,)), dma((NZ,)), dma((NZ,)),
            dma((NZ,)), dma((NZ,)), dma((NZ,)), dma((NZ,)),
            dma((NZ, 4)), dma,
        ],
        compiler_params=pltpu.CompilerParams(
            collective_id=0, has_side_effects=True, vmem_limit_bytes=62 * 2**20),
        name="attention_tangent",
    )(*arrays))


def solution(mesh):
    rows_in = P(("batch", "blk"), "head")
    rows_out = P(("batch", "blk", "head"), None)
    return jax.shard_map(
        local, mesh=mesh, in_specs=(rows_in,) * 6, out_specs=(rows_out, rows_out), check_vma=False,
    )
```

time: 152 us -> 99.2 us (0.65); the launches traced: 149 us -> 99.1 us
  Pallas kernels: 141 us -> 95.9 us
  local copies, waits for them, and re-layouts: 7.46 us -> 2.57 us
    pallas_call x1, Pallas kernels: 141 us -> 95.9 us  [local(): pl.pallas_call(functools.partial(kernel, rows), out_shape=(out, out), in_...]
    unnamed x14 -> x4, local copies, waits for them, and re-layouts: 7.46 us -> 2.57 us
where the time goes in v2:
time: 99.2 us; the launch traced here: 99.1 us
  Pallas kernels  95.9 us (97%)
  local copies, waits for them, and re-layouts  2.57 us (3%)
    pallas_call x1, Pallas kernels, local(): pl.pallas_call(functools.partial(kernel, rows), out_shape=(out, out), in_...  95.9 us
    unnamed x4, local copies, waits for them, and re-layouts  2.57 us

profile of v2, /device:TPU:1, one launch (start us, length us, event | category | flops | bytes accessed | tf_op | source)
XLA Modules:
  0.0 99.1 jit_solution(11465110025320926961)
XLA Ops:
  0.6 95.9 %attention_tangent.1 = (bf16[64,3072]{1,0:T(8,128)(2,1)}, bf16[64,3072]{1,0:T(8,128)(2,1)}) custom-call(bf16[256,768]{1,0:T(8,128)(2,1)} %q_in.1, bf16[256,768]{1,0:T(8,128)(2,1)} %k_in.1, bf16[256,768]{1,0:T(8,128)(2,1)} %v_in.1, bf16[256,768]{1,0:T(8,128)(2,1)} %qt_in.1, bf16[256,768]{1,0:T(8,128)(2,1)} %kt_in.1, bf16[256,768]{1,0:T(8,128)(2,1)} %vt_in.1), custom_call_target="tpu_custom_call" | custom-call | tf_op jit(solution)/shard_map/attention_tangent/pallas_call | solution.py:230
  96.5 0.0 copy-start
  96.5 1.8 %copy.10 = bf16[64,3072]{1,0:T(8,128)(2,1)} copy(bf16[64,3072]{1,0:T(8,128)(2,1)} %get-tuple-element.4) | data formatting | bytes 786432
  98.3 0.0 copy-done
  98.3 0.7 copy.11
Async XLA Ops:
  96.5 1.8 %copy-start = (bf16[64,3072]{1,0:T(8,128)(2,1)S(1)}, bf16[64,3072]{1,0:T(8,128)(2,1)}, u32[]{:S(2)}) copy-start(bf16[64,3072]{1,0:T(8,128)(2,1)} %get-tuple-element.5) | copy-start | bytes 1179652

commit v3 on v2

--- a/solution.py
+++ b/solution.py
@@ -13,6 +13,8 @@
 NT = (((1,), (1,)), ((), ()))
 
 NZ = 8
+QUERIES, KEYS = (0, 1), (2, 3, 4, 5)
+RELAYED = (0, 2, 3)
 MANY = 2048
 OWN = 6
 
@@ -28,9 +30,9 @@
 
 
 def kernel(
-    rows, q_in, k_in, v_in, qt_in, kt_in, vt_in, o_ref, ot_ref,
-    qq, kk, vv, res, got,
-    send_in, got_q, got_k, got_v, pass_k, pass_v, come_k, come_v, send_out, got_out,
+    rows, q_in, k_in, v_in, qt_in, kt_in, vt_in, got,
+    qq, kk, vv, res, relay,
+    send_in, got_q, got_k, got_v, pass_k, pass_v, come_k, come_v, send_out, got_out, relay_in, relay_out,
 ):
     quarter = rows // 4
     blk, head, y = lax.axis_index("blk"), lax.axis_index("head"), lax.axis_index("batch")
@@ -59,29 +61,39 @@
 
     for other in range(1, 4):
         greet(blk, lax.rem(head + other, 4))
-    pl.semaphore_wait(barrier, OWN + 3 - jnp.where(at_home, 1, 0))
+    partner = lax.rem(z + 2 * lax.rem(z, 2) + NZ - 1, NZ)
+    greet(2 * partner + s, head)
+    pl.semaphore_wait(barrier, OWN + 4 - jnp.where(at_home, 1, 0))
 
     sources = (qt_in, q_in, k_in, kt_in, v_in, vt_in)
     turn = 1 - 2 * core
 
     def owner_at(n):
-        zo = lax.rem(z + step_of(n, turn) + NZ, NZ)
+        return owner_on(lax.rem(z + step_of(n, turn) + NZ, NZ))
+
+    def owner_on(zo):
         there = lax.rem(zo + NZ - 2 * core, NZ)
         return zo, there - there // 4, lax.rem(there, 4) != 3
 
     def slot(n, side):
         return pl.ds(pl.multiple_of((2 * n + side) * rows, rows), rows)
+
+    def place_of(n, a):
+        half = slice(HD * (a % 2), HD * (a % 2 + 1))
+        if a < 2:
+            return qq.at[n * rows:(n + 1) * rows, half], got_q.at[n]
+        if a < 4:
+            return kk.at[slot(n, s), half], got_k.at[n]
+        return vv.at[slot(n, s), half], got_v.at[n]
 
     def send(n, a):
         zo, i, owns = owner_at(n)
         src = sources[a].at[:, pl.ds(pl.multiple_of(i * HD, HD), HD)]
-        half = slice(HD * (a % 2), HD * (a % 2 + 1))
-        if a < 2:
-            dst, got_sem = qq.at[n * rows:(n + 1) * rows, half], got_q.at[n]
-        elif a < 4:
-            dst, got_sem = kk.at[slot(n, s), half], got_k.at[n]
-        else:
-            dst, got_sem = vv.at[slot(n, s), half], got_v.at[n]
+        dst, got_sem = place_of(n, a)
+        to = device(2 * zo + core, 2 * x_hi + s)
+        if n == 1 and a in RELAYED:
+            r = RELAYED.index(a)
+            dst, got_sem, to = relay.at[r], relay_in.at[r], device(2 * partner + s, head)
 
         def local():
             pltpu.make_async_copy(src, dst, got_sem).start()
@@ -89,7 +101,7 @@
         def remote():
             pltpu.make_async_remote_copy(
                 src_ref=src, dst_ref=dst, send_sem=send_in.at[a, i], recv_sem=got_sem,
-                device_id=device(2 * zo + core, 2 * x_hi + s), device_id_type=MESH,
+                device_id=to, device_id_type=MESH,
             ).start()
 
         if n == 0:
@@ -98,11 +110,44 @@
         else:
             pl.when(owns)(remote)
 
-    for kinds, steps in (((0, 1), (0,)), ((2, 3, 4, 5), (0, 2, 4, 6)), ((0, 1), (2, 4, 6))):
+    def send_all(kinds, steps):
         for n in steps:
             for a in kinds:
                 send(n, a)
                 send(n + 1, a)
+
+    def sent(kinds):
+        for n in range(NZ):
+            zo, i, owns = owner_at(n)
+            src = q_in.at[:, pl.ds(pl.multiple_of(i * HD, HD), HD)]
+
+            @pl.when(jnp.logical_and(owns, s != core) if n == 0 else owns)
+            def _():
+                for a in kinds:
+                    pltpu.make_async_copy(src, src, send_in.at[a, i]).wait()
+
+    send_all(QUERIES, (0,))
+    send_all(KEYS, (0, 2, 4, 6))
+
+    zo_partner, _, relays = owner_on(lax.rem(partner + NZ // 2, NZ))
+
+    def pass_on(r):
+        dst, got_sem = place_of(1, RELAYED[r])
+        return pltpu.make_async_remote_copy(
+            src_ref=relay.at[r], dst_ref=dst, send_sem=relay_out.at[r], recv_sem=got_sem,
+            device_id=device(2 * zo_partner + core, 2 * x_hi + s), device_id_type=MESH,
+        )
+
+    @pl.when(relays)
+    def _():
+        for r in range(len(RELAYED)):
+            pltpu.make_async_copy(relay.at[r], relay.at[r], relay_in.at[r]).wait()
+            pass_on(r).start()
+
+    @pl.when(jnp.logical_not(active))
+    def _():
+        sent(KEYS)
+        send_all(QUERIES, (2, 4, 6))
 
     scaling = HD ** -0.5
     factor = scaling * LOG2E
@@ -184,6 +229,8 @@
             landed(vv.at[slot(n, core), :], got_v.at[n])
             to_sibling(n, vv, pass_v, come_v).start()
 
+        send_all(QUERIES, (2, 4, 6))
+
         @pl.loop(0, NZ)
         def _(n):
             landed(kk.at[slot(n, 1 - core), :], come_k.at[n])
@@ -195,17 +242,17 @@
             attend(n)
             send_result(n)
 
-    for n in range(NZ):
-        zo, i, owns = owner_at(n)
-        src = q_in.at[:, pl.ds(pl.multiple_of(i * HD, HD), HD)]
-
-        @pl.when(jnp.logical_and(owns, s != core) if n == 0 else owns)
-        def _():
-            for a in range(6):
-                landed(src, send_in.at[a, i])
+    sent(QUERIES)
+
+    @pl.when(relays)
+    def _():
+        for r in range(len(RELAYED)):
+            pass_on(r).wait_send()
 
     @pl.when(active)
     def _():
+        sent(KEYS)
+
         @pl.loop(0, NZ)
         def _(n):
             landed(kk.at[slot(n, core), :], pass_k.at[n])
@@ -216,36 +263,33 @@
                     landed(res.at[n, part], send_out.at[n, part])
 
     landed(got, got_out)
-    for h in range(4 * OWN):
-        o_ref[:, h * HD:(h + 1) * HD] = got[h, 0]
-        ot_ref[:, h * HD:(h + 1) * HD] = got[h, 1]
 
 
 def local(*arrays):
     rows = arrays[0].shape[0]
-    out = jax.ShapeDtypeStruct((rows // 4, 24 * HD), jnp.bfloat16)
     queries = NZ * rows
     bf16 = jnp.bfloat16
     dma = pltpu.SemaphoreType.DMA
-    return tuple(pl.pallas_call(
+    got = pl.pallas_call(
         functools.partial(kernel, rows),
-        out_shape=(out, out),
+        out_shape=jax.ShapeDtypeStruct((4 * OWN, 2, rows // 4, HD), bf16),
         in_specs=[pl.BlockSpec(memory_space=pltpu.HBM)] * 6,
-        out_specs=(pl.BlockSpec(memory_space=pltpu.VMEM),) * 2,
+        out_specs=pl.BlockSpec(memory_space=pltpu.HBM),
         scratch_shapes=[
             pltpu.VMEM((queries, 2 * HD), bf16),
             pltpu.VMEM((2 * queries, 2 * HD), bf16),
             pltpu.VMEM((2 * queries, 2 * HD), bf16),
             pltpu.VMEM((NZ, 4, 2, rows // 4, HD), bf16),
-            pltpu.VMEM((4 * OWN, 2, rows // 4, HD), bf16),
+            pltpu.VMEM((len(RELAYED), rows, HD), bf16),
             dma((6, OWN)), dma((NZ,)), dma((NZ,)), dma((NZ,)),
             dma((NZ,)), dma((NZ,)), dma((NZ,)), dma((NZ,)),
-            dma((NZ, 4)), dma,
+            dma((NZ, 4)), dma, dma((len(RELAYED),)), dma((len(RELAYED),)),
         ],
         compiler_params=pltpu.CompilerParams(
             collective_id=0, has_side_effects=True, vmem_limit_bytes=62 * 2**20),
         name="attention_tangent",
-    )(*arrays))
+    )(*arrays)
+    return tuple(got[:, a].transpose(1, 0, 2).reshape(rows // 4, -1) for a in range(2))
 
 
 def solution(mesh):

time: 99.2 us -> 92.1 us (0.928)
  Pallas kernels: 95.9 us -> 89.2 us
    pallas_call x1, Pallas kernels: 95.9 us -> 89.2 us  [local(): pl.pallas_call(functools.partial(kernel, rows), out_shape=jax.ShapeDtypeS...]
    unnamed x4 -> x1, local copies, waits for them, and re-layouts: 2.57 us -> 1.18 us
    reshape x0 -> x1, local copies, waits for them, and re-layouts: none -> 0.99 us  [local(): got[:, a].transpose(1, 0, 2).reshape(rows // 4, -1)]
where the time goes in v3:
time: 92.1 us; the launch traced here: 92 us
  Pallas kernels  89.2 us (97%)
  local copies, waits for them, and re-layouts  2.17 us (2%)
    pallas_call x1, Pallas kernels, local(): pl.pallas_call(functools.partial(kernel, rows), out_shape=jax.ShapeDtypeS...  89.2 us

profile of v3, /device:TPU:1, one launch (start us, length us, event | category | flops | bytes accessed | tf_op | source)
XLA Modules:
  0.0 92.0 jit_solution(5167640645689233718)
XLA Ops:
  0.6 89.2 %attention_tangent.1 = bf16[24,2,64,128]{3,2,1,0:T(8,128)(2,1)} custom-call(bf16[256,768]{1,0:T(8,128)(2,1)} %q_in.1, bf16[256,768]{1,0:T(8,128)(2,1)} %k_in.1, bf16[256,768]{1,0:T(8,128)(2,1)} %v_in.1, bf16[256,768]{1,0:T(8,128)(2,1)} %qt_in.1, bf16[256,768]{1,0:T(8,128)(2,1)} %kt_in.1, bf16[256,768]{1,0:T(8,128)(2,1)} %vt_in.1), custom_call_target="tpu_custom_call" | custom-call | tf_op jit(solution)/shard_map/attention_tangent/pallas_call | solution.py:273
  89.8 1.2 %slice_bitcast_fusion = (bf16[24,8,8,128]{3,2,1,0:T(8,128)(2,1)S(1)}, bf16[24,8,8,128]{3,2,1,0:T(8,128)(2,1)S(1)}) fusion(bf16[24,2,64,128]{3,2,1,0:T(8,128)(2,1)} %attention_tangent.1), kind=kLoop, calls=%fused_computation.2 | loop fusion | bytes 1572864
  91.0 1.0 %copy_bitcast_fusion = (bf16[64,3072]{1,0:T(8,128)(2,1)}, bf16[64,3072]{1,0:T(8,128)(2,1)}) fusion(bf16[24,8,8,128]{3,2,1,0:T(8,128)(2,1)S(1)} %get-tuple-element.2, bf16[24,8,8,128]{3,2,1,0:T(8,128)(2,1)S(1)} %get-tuple-element.3), kind=kLoop, calls=%fused_computation | loop fusion | bytes 1572864 | tf_op jit(solution)/shard_map/reshape | solution.py:292

commit v4 on v3

--- a/solution.py
+++ b/solution.py
@@ -14,6 +14,7 @@
 
 NZ = 8
 QUERIES, KEYS = (0, 1), (2, 3, 4, 5)
+EARLY, LATE = ((0,), (1,)), ((2, 3), (4, 5), (6, 7))
 RELAYED = (0, 2, 3)
 MANY = 2048
 OWN = 6
@@ -111,10 +112,10 @@
             pl.when(owns)(remote)
 
     def send_all(kinds, steps):
-        for n in steps:
+        for some in steps:
             for a in kinds:
-                send(n, a)
-                send(n + 1, a)
+                for n in some:
+                    send(n, a)
 
     def sent(kinds):
         for n in range(NZ):
@@ -126,8 +127,8 @@
                 for a in kinds:
                     pltpu.make_async_copy(src, src, send_in.at[a, i]).wait()
 
-    send_all(QUERIES, (0,))
-    send_all(KEYS, (0, 2, 4, 6))
+    send_all(QUERIES, EARLY)
+    send_all(KEYS, ((0, 1), (2, 3), (4, 5), (6, 7)))
 
     zo_partner, _, relays = owner_on(lax.rem(partner + NZ // 2, NZ))
 
@@ -138,16 +139,21 @@
             device_id=device(2 * zo_partner + core, 2 * x_hi + s), device_id_type=MESH,
         )
 
-    @pl.when(relays)
-    def _():
-        for r in range(len(RELAYED)):
-            pltpu.make_async_copy(relay.at[r], relay.at[r], relay_in.at[r]).wait()
-            pass_on(r).start()
+    def relay_all(kinds):
+        @pl.when(relays)
+        def _():
+            for r, a in enumerate(RELAYED):
+                if a in kinds:
+                    pltpu.make_async_copy(relay.at[r], relay.at[r], relay_in.at[r]).wait()
+                    pass_on(r).start()
+
+    relay_all(QUERIES + KEYS)
 
     @pl.when(jnp.logical_not(active))
     def _():
         sent(KEYS)
-        send_all(QUERIES, (2, 4, 6))
+        send_all(QUERIES, LATE)
+
 
     scaling = HD ** -0.5
     factor = scaling * LOG2E
@@ -198,7 +204,7 @@
     def landed(ref, sem):
         pltpu.make_async_copy(ref, ref, sem).wait()
 
-    column0 = (2 * x_hi + s) * OWN + mine
+    columns = pl.ds(pl.multiple_of(((2 * x_hi + s) * OWN + mine) * HD, HD), HD)
 
     def row_home(n):
         return 2 * lax.rem(z - step_at(n, 1 - 2 * s) + NZ, NZ) + core
@@ -206,7 +212,7 @@
     def send_result(n):
         home = row_home(n)
         for part in range(4):
-            src, dst = res.at[n, part], got.at[column0]
+            src, dst = res.at[n, part], got.at[:, :, columns]
             here = jnp.logical_and(home == blk, head == part)
 
             @pl.when(here)
@@ -222,14 +228,15 @@
 
     @pl.when(active)
     def _():
-        @pl.loop(0, NZ)
-        def _(n):
+        def arrive(n):
             landed(kk.at[slot(n, core), :], got_k.at[n])
             to_sibling(n, kk, pass_k, come_k).start()
             landed(vv.at[slot(n, core), :], got_v.at[n])
             to_sibling(n, vv, pass_v, come_v).start()
 
-        send_all(QUERIES, (2, 4, 6))
+        pl.loop(0, 5)(arrive)
+        send_all(QUERIES, LATE)
+        pl.loop(5, NZ)(arrive)
 
         @pl.loop(0, NZ)
         def _(n):
@@ -272,7 +279,7 @@
     dma = pltpu.SemaphoreType.DMA
     got = pl.pallas_call(
         functools.partial(kernel, rows),
-        out_shape=jax.ShapeDtypeStruct((4 * OWN, 2, rows // 4, HD), bf16),
+        out_shape=jax.ShapeDtypeStruct((2, rows // 4, 4 * OWN * HD), bf16),
         in_specs=[pl.BlockSpec(memory_space=pltpu.HBM)] * 6,
         out_specs=pl.BlockSpec(memory_space=pltpu.HBM),
         scratch_shapes=[
@@ -289,7 +296,7 @@
             collective_id=0, has_side_effects=True, vmem_limit_bytes=62 * 2**20),
         name="attention_tangent",
     )(*arrays)
-    return tuple(got[:, a].transpose(1, 0, 2).reshape(rows // 4, -1) for a in range(2))
+    return got[0], got[1]
 
 
 def solution(mesh):

time: 92.1 us -> 91 us (0.988)
  Pallas kernels: 89.2 us -> 88.2 us
    squeeze x0 -> x1, local copies, waits for them, and re-layouts: none -> 2.04 us  [local(): return (got[0], got[1])]
    unnamed x1 -> x0, local copies, waits for them, and re-layouts: 1.18 us -> none
    pallas_call x1, Pallas kernels: 89.2 us -> 88.2 us  [local(): pl.pallas_call(functools.partial(kernel, rows), out_shape=jax.ShapeDtypeS...]
    reshape x1 -> x0, local copies, waits for them, and re-layouts: 0.99 us -> none  [local(): got[:, a].transpose(1, 0, 2).reshape(rows // 4, -1)]
where the time goes in v4:
time: 91 us; the launch traced here: 90.8 us
  Pallas kernels  88.2 us (97%)
  local copies, waits for them, and re-layouts  2.04 us (2%)
    pallas_call x1, Pallas kernels, local(): pl.pallas_call(functools.partial(kernel, rows), out_shape=jax.ShapeDtypeS...  88.2 us
    squeeze x1, local copies, waits for them, and re-layouts, local(): return (got[0], got[1])  2.04 us

profile of v4, /device:TPU:1, one launch (start us, length us, event | category | flops | bytes accessed | tf_op | source)
XLA Modules:
  0.0 90.8 jit_solution(13097202297430387768)
XLA Ops:
  0.6 88.2 %attention_tangent.1 = bf16[2,64,3072]{2,1,0:T(8,128)(2,1)} custom-call(bf16[256,768]{1,0:T(8,128)(2,1)} %q_in.1, bf16[256,768]{1,0:T(8,128)(2,1)} %k_in.1, bf16[256,768]{1,0:T(8,128)(2,1)} %v_in.1, bf16[256,768]{1,0:T(8,128)(2,1)} %qt_in.1, bf16[256,768]{1,0:T(8,128)(2,1)} %kt_in.1, bf16[256,768]{1,0:T(8,128)(2,1)} %vt_in.1), custom_call_target="tpu_custom_call" | custom-call | tf_op jit(solution)/shard_map/attention_tangent/pallas_call | solution.py:280
  88.8 2.0 %slice_bitcast_fusion = (bf16[64,3072]{1,0:T(8,128)(2,1)}, bf16[64,3072]{1,0:T(8,128)(2,1)}) fusion(bf16[2,64,3072]{2,1,0:T(8,128)(2,1)} %attention_tangent.1), kind=kLoop, calls=%fused_computation | loop fusion | bytes 1572864 | tf_op jit(solution)/shard_map/squeeze | solution.py:299

commit v5 on v4

--- a/solution.py
+++ b/solution.py
@@ -117,8 +117,8 @@
                 for n in some:
                     send(n, a)
 
-    def sent(kinds):
-        for n in range(NZ):
+    def sent(kinds, steps=range(NZ)):
+        for n in steps:
             zo, i, owns = owner_at(n)
             src = q_in.at[:, pl.ds(pl.multiple_of(i * HD, HD), HD)]
 
@@ -152,8 +152,9 @@
     @pl.when(jnp.logical_not(active))
     def _():
         sent(KEYS)
-        send_all(QUERIES, LATE)
-
+        for some in LATE:
+            send_all(QUERIES, (some,))
+            sent(QUERIES, some)
 
     scaling = HD ** -0.5
     factor = scaling * LOG2E
@@ -234,9 +235,9 @@
             landed(vv.at[slot(n, core), :], got_v.at[n])
             to_sibling(n, vv, pass_v, come_v).start()
 
-        pl.loop(0, 5)(arrive)
-        send_all(QUERIES, LATE)
-        pl.loop(5, NZ)(arrive)
+        pl.loop(0, 7)(arrive)
+        send_all(QUERIES, LATE[:1])
+        pl.loop(7, NZ)(arrive)
 
         @pl.loop(0, NZ)
         def _(n):
@@ -245,11 +246,14 @@
 
         @pl.loop(0, NZ)
         def _(n):
+            for k in range(1, len(LATE)):
+                pl.when(n == 2 * k - 2)(functools.partial(send_all, QUERIES, (LATE[k],)))
             landed(qq.at[pl.ds(pl.multiple_of(n * rows, rows), rows), :], got_q.at[n])
             attend(n)
             send_result(n)
 
-    sent(QUERIES)
+    pl.when(active)(lambda: sent(QUERIES))
+    pl.when(jnp.logical_not(active))(lambda: sent(QUERIES, sum(EARLY, ())))
 
     @pl.when(relays)
     def _():

time: 91 us -> 90.7 us (level)
  no operation moved by 1% of the time
where the time goes in v5:
time: 90.7 us; the launch traced here: 90.1 us
  Pallas kernels  87.5 us (96%)
  local copies, waits for them, and re-layouts  2.04 us (2%)
    pallas_call x1, Pallas kernels, local(): pl.pallas_call(functools.partial(kernel, rows), out_shape=jax.ShapeDtypeS...  87.5 us
    squeeze x1, local copies, waits for them, and re-layouts, local(): return (got[0], got[1])  2.04 us

profile of v5, /device:TPU:1, one launch (start us, length us, event | category | flops | bytes accessed | tf_op | source)
XLA Modules:
  0.0 90.1 jit_solution(651702642734298808)
XLA Ops:
  0.6 87.5 %attention_tangent.1 = bf16[2,64,3072]{2,1,0:T(8,128)(2,1)} custom-call(bf16[256,768]{1,0:T(8,128)(2,1)} %q_in.1, bf16[256,768]{1,0:T(8,128)(2,1)} %k_in.1, bf16[256,768]{1,0:T(8,128)(2,1)} %v_in.1, bf16[256,768]{1,0:T(8,128)(2,1)} %qt_in.1, bf16[256,768]{1,0:T(8,128)(2,1)} %kt_in.1, bf16[256,768]{1,0:T(8,128)(2,1)} %vt_in.1), custom_call_target="tpu_custom_call" | custom-call | tf_op jit(solution)/shard_map/attention_tangent/pallas_call | solution.py:284
  88.1 2.0 %slice_bitcast_fusion = (bf16[64,3072]{1,0:T(8,128)(2,1)}, bf16[64,3072]{1,0:T(8,128)(2,1)}) fusion(bf16[2,64,3072]{2,1,0:T(8,128)(2,1)} %attention_tangent.1), kind=kLoop, calls=%fused_computation | loop fusion | bytes 1572864 | tf_op jit(solution)/shard_map/squeeze | solution.py:303
